TPU v7x, 256 devices: a whole 4x4x8 slice. The times are simulated.
256 devices in a mesh: pair: 8 (over x_lo, y), outv: 8 (over z), conv: 4 (over x_hi, core).
Axes of the slice: x: 4 (x_hi: 2, x_lo: 2; x = x_hi * 2 + x_lo), y: 4, z: 8, core: 2. Of those that a mesh axis runs over, the one named last changes fastest.
Arguments:
- amplitudes: bfloat16 [16384, 6144], P('pair', ('conv', 'outv')), may hold values from -6 to 6
- integrals: bfloat16 [6144, 12288], P('conv', ('outv', 'pair')), may hold values from -0.21875 to 0.21875
- amp_mask: int32 [8, 64], P('pair', 'conv'), may hold values from 0 to 1, as said below
- int_mask: int32 [64, 128], P('conv', 'outv'), may hold values 0 or 1
Outputs:
- ladder: bfloat16 [12288, 16384], P(('outv', 'conv'), 'pair')
Inputs may be any that keep to these rules, and one draw needn't show every extreme that they name: `amp_mask`: 0 or 1; the share of ones differs from pair tile to pair tile.
All inputs are finite; a program needn't handle non-finite values. No bound on the sum of `int_mask` on one device may be relied on, other than what follows from the above.
Results may differ from a plain program's by a relative error of at most 0.001.
Values may be sent and summed in bfloat16 or wider, within the bound.
No kernel may reach another device: no remote copies, remote signals or barrier semaphores. Data moves between devices by JAX's collectives and lax.ppermute only.
A program may use at most 64 MiB of HBM per device.

v0:
```python
import jax
import jax.numpy as jnp
from jax import lax
from jax.sharding import PartitionSpec as P

TW = 96


def column_mask(block_mask, first, width):
    tiles = block_mask.shape[1]
    col_tile = (first * width + jnp.arange(width, dtype=jnp.int32)) // TW
    onehot = (col_tile[None, :] == jnp.arange(tiles, dtype=jnp.int32)[:, None]).astype(jnp.float32)
    return jnp.dot(block_mask.astype(jnp.float32), onehot, preferred_element_type=jnp.float32)


def contract(columns, amp_rows):
    dims = (((0,), (1,)), ((), ()))
    return lax.dot_general(columns, amp_rows, dims, preferred_element_type=jnp.float32)


def body(amplitudes, integrals, amp_mask, int_mask):
    width_amp = amplitudes.shape[1]
    amp_cols = column_mask(amp_mask, lax.axis_index("outv"), width_amp)
    amp_local = amplitudes * amp_cols.astype(jnp.bfloat16)
    amp_rows = lax.all_gather(amp_local, "outv", axis=1, tiled=True)
    tiles_k = int_mask.shape[0]
    width_int = integrals.shape[1]
    int_cols = column_mask(int_mask, lax.axis_index("pair"), width_int)
    int_local = (
        integrals.reshape(tiles_k, TW, width_int) * int_cols[:, None, :].astype(jnp.bfloat16)
    ).reshape(tiles_k * TW, width_int)
    int_full = lax.all_gather(int_local, "pair", axis=1, tiled=True)
    summed = lax.psum_scatter(contract(int_full, amp_rows), "conv", scatter_dimension=0, tiled=True)
    return summed.astype(jnp.bfloat16)


def solution(mesh):
    placed = (
        P("pair", ("conv", "outv")),
        P("conv", ("outv", "pair")),
        P("pair", "conv"),
        P("conv", "outv"),
    )
    return jax.shard_map(
        body, mesh=mesh, in_specs=placed, out_specs=P(("outv", "conv"), "pair"), check_vma=False
    )
```

profile of v0, /device:TPU:1, one launch (start us, length us, event | category | flops | bytes accessed | tf_op | source)
XLA Modules:
  0.0 285.8 jit_solution(13967554948303165017)
XLA Ops:
  6.5 0.0 all-gather.3.cloned.1.call-start
  6.6 0.8 fusion
  7.4 0.1 copy.5
  7.5 0.5 mul.26
  8.0 0.9 mul.27
  8.9 2.0 mul.28
  10.9 0.0 all-gather.3.cloned.1.call-update
  10.9 0.0 all-gather.5.cloned.1.call-start
  11.0 0.8 fusion.1
  11.8 2.1 broadcast_multiply_fusion
  13.9 0.0 all-gather.5.cloned.1.call-update
  13.9 0.0 reduce-scatter.2.cloned.1.call-start
  14.0 61.0 %all-gather.3.cloned.1.call-done = bf16[1536,1536]{0,1:T(8,128)(2,1)} async-done(((bf16[1536,192]{0,1:T(8,128)(2,1)}), bf16[1536,1536]{0,1:T(8,128)(2,1)}) %all-gather.3.cloned.1.call-update) | async-done | bytes 4718608 | tf_op jit(solution)/shard_map/all_gather | solution.py:32
  75.0 75.1 %all-gather.5.cloned.1.call-done = bf16[2048,1536]{0,1:T(8,128)(2,1)} async-done(((bf16[2048,192]{0,1:T(8,128)(2,1)}), bf16[2048,1536]{0,1:T(8,128)(2,1)}) %all-gather.5.cloned.1.call-update) | async-done | bytes 6291472 | tf_op jit(solution)/shard_map/all_gather | solution.py:25
  150.1 16.1 %fusion.5 = f32[1536,2048]{1,0:T(8,128)} fusion(bf16[1536,1536]{0,1:T(8,128)(2,1)} %all-gather.3.cloned.1.call-done, bf16[2048,1536]{0,1:T(8,128)(2,1)} %all-gather.5.cloned.1.call-done), kind=kOutput, calls=%fused_computation.12 | convolution fusion | flops 9663676416 | bytes 23592960 | tf_op jit(solution)/shard_map/dot_general | solution.py:18
  166.2 0.0 reduce-scatter.2.cloned.1.call-update
  166.2 109.8 %reduce-scatter.2.cloned.1.call-done = f32[384,2048]{1,0:T(8,128)} async-done(((f32[1536,2048]{1,0:T(8,128)}), f32[384,2048]{1,0:T(8,128)}) %reduce-scatter.2.cloned.1.call-update) | async-done | bytes 3145744 | tf_op jit(solution)/shard_map/reduce_scatter | solution.py:33
  276.0 3.3 %convert_element_type.27 = bf16[384,2048]{1,0:T(8,128)(2,1)} convert(f32[384,2048]{1,0:T(8,128)} %reduce-scatter.2.cloned.1.call-done) | non-fusion elementwise | flops 786432 | bytes 4718592 | tf_op jit(solution)/shard_map/convert_element_type | solution.py:34
  (3 shorter events, 0.0 us)
Async XLA Ops:
  6.5 68.4 %all-gather.3.cloned.1.call-start = ((), (), s32[]{:S(2)}) async-start(), calls=%async_computation.1 | async-start | bytes 5308416 | tf_op jit(solution)/shard_map/all_gather | solution.py:32
  10.9 139.1 %all-gather.5.cloned.1.call-start = ((), (), s32[]{:S(2)}) async-start(), calls=%async_computation.2 | async-start | bytes 7077888 | tf_op jit(solution)/shard_map/all_gather | solution.py:25
  13.9 262.1 %reduce-scatter.2.cloned.1.call-start = ((), (), s32[]{:S(2)}) async-start(), calls=%async_computation.3 | async-start | bytes 15728640 | tf_op jit(solution)/shard_map/reduce_scatter | solution.py:33
Sparse Core Ops, SparseCore 0:
  11.0 63.8 all-gather.2
  76.7 73.2 all-gather.4
  166.3 109.6 reduce-scatter.1
where the time goes:
time: 286 us
  waiting for transfers between devices  246 us (86%)
  matrix products  17.7 us (6%)
  between operations  13.1 us (5%)
  other arithmetic  7.46 us (3%)
    reduce_scatter x1, waiting for transfers between devices, body(): lax.psum_scatter(contract(int_full, amp_rows), 'conv', scatter_dimension=...  110 us
    all_gather x1, waiting for transfers between devices, body(): amp_rows = lax.all_gather(amp_local, 'outv', axis=1, tiled=True)  75.1 us
    all_gather x1, waiting for transfers between devices, body(): int_full = lax.all_gather(int_local, 'pair', axis=1, tiled=True)  61 us
    dot_general x1, matrix products, contract(): lax.dot_general(columns, amp_rows, dims, preferred_element_type=jnp.float32)  16.1 us
  transfers between devices with their start and end apart: 3, of which 3 were waited for; matrix products, arithmetic and copies ran while one was open for 1% of the time, Pallas kernels for 0%

commit v1 on v0

--- a/solution.py
+++ b/solution.py
@@ -22,7 +22,8 @@
     width_amp = amplitudes.shape[1]
     amp_cols = column_mask(amp_mask, lax.axis_index("outv"), width_amp)
     amp_local = amplitudes * amp_cols.astype(jnp.bfloat16)
-    amp_rows = lax.all_gather(amp_local, "outv", axis=1, tiled=True)
+    copies = jnp.concatenate([amp_local] * lax.axis_size("outv"), axis=1)
+    amp_rows = lax.all_to_all(copies, "outv", 1, 1, tiled=True)
     tiles_k = int_mask.shape[0]
     width_int = integrals.shape[1]
     int_cols = column_mask(int_mask, lax.axis_index("pair"), width_int)

time: 286 us -> 301 us (1.052)
  starting transfers between devices: 0.09 us -> 9.22 us
    all_to_all x0 -> x1, waiting for transfers between devices: none -> 77.1 us  [body(): amp_rows = lax.all_to_all(copies, 'outv', 1, 1, tiled=True)]
    all_gather x1 -> x0, waiting for transfers between devices: 75.1 us -> none  [body(): amp_rows = lax.all_gather(amp_local, 'outv', axis=1, tiled=True)]
    all_to_all x0 -> x1, starting transfers between devices: none -> 9.15 us  [body(): amp_rows = lax.all_to_all(copies, 'outv', 1, 1, tiled=True)]
    unnamed x0 -> x7, other arithmetic: none -> 5.93 us
where the time goes in v1:
time: 301 us
  waiting for transfers between devices  247 us (82%)
  matrix products  17 us (6%)
  between operations  13.5 us (4%)
  other arithmetic  10.4 us (3%)
  starting transfers between devices  9.22 us (3%)
  local copies, waits for them, and re-layouts  4.15 us (1%)
    reduce_scatter x1, waiting for transfers between devices, body(): lax.psum_scatter(contract(int_full, amp_rows), 'conv', scatter_dimension=...  107 us
    all_to_all x1, waiting for transfers between devices, body(): amp_rows = lax.all_to_all(copies, 'outv', 1, 1, tiled=True)  77.1 us
    all_gather x1, waiting for transfers between devices, body(): int_full = lax.all_gather(int_local, 'pair', axis=1, tiled=True)  62.1 us
    dot_general x1, matrix products, contract(): lax.dot_general(columns, amp_rows, dims, preferred_element_type=jnp.float32)  16 us
    all_to_all x1, starting transfers between devices, body(): amp_rows = lax.all_to_all(copies, 'outv', 1, 1, tiled=True)  9.15 us
  transfers between devices with their start and end apart: 3, of which 3 were waited for; matrix products, arithmetic and copies ran while one was open for 1% of the time, Pallas kernels for 0%

profile of v1, /device:TPU:1, one launch (start us, length us, event | category | flops | bytes accessed | tf_op | source)
XLA Modules:
  0.0 300.9 jit_solution(13848429879386298907)
XLA Ops:
  6.5 0.9 fusion.1
  7.4 1.3 constant_dynamic-update-slice_fusion.7
  8.7 1.3 constant_dynamic-update-slice_fusion.6
  10.1 1.3 constant_dynamic-update-slice_fusion.5
  11.4 1.3 constant_dynamic-update-slice_fusion.4
  12.8 0.2 constant_dynamic-update-slice_fusion.3
  13.0 0.2 constant_dynamic-update-slice_fusion.2
  13.2 0.2 constant_dynamic-update-slice_fusion.1
  13.4 0.2 constant_dynamic-update-slice_fusion
  13.6 2.7 copy-done.1
  16.2 9.1 %all-to-all-start = ((bf16[2048,8,192]{0,2,1:T(8,128)(2,1)}), bf16[2048,8,192]{0,2,1:T(8,128)(2,1)}, u32[]{:S(2)}, u32[]{:S(2)}) async-start(bf16[2048,8,192]{0,2,1:T(8,128)(2,1)} %bitcast.13), calls=%async_computation | async-start | bytes 12582912 | tf_op jit(solution)/shard_map/all_to_all | solution.py:26
  25.4 0.0 all-gather.2.cloned.1.call-start
  25.5 0.1 fusion
  25.6 0.1 copy.5
  25.7 0.5 mul.26
  26.2 0.9 mul.27
  27.1 1.0 mul.28
  28.0 0.0 all-gather.2.cloned.1.call-update
  28.1 0.0 reduce-scatter.2.cloned.1.call-start
  28.1 62.1 %all-gather.2.cloned.1.call-done = bf16[1536,1536]{0,1:T(8,128)(2,1)} async-done(((bf16[1536,192]{0,1:T(8,128)(2,1)}), bf16[1536,1536]{0,1:T(8,128)(2,1)}) %all-gather.2.cloned.1.call-update) | async-done | bytes 4718608 | tf_op jit(solution)/shard_map/all_gather | solution.py:33
  90.2 77.1 %all-to-all-done = bf16[2048,8,192]{0,2,1:T(8,128)(2,1)} async-done(((bf16[2048,8,192]{0,2,1:T(8,128)(2,1)}), bf16[2048,8,192]{0,2,1:T(8,128)(2,1)}, u32[]{:S(2)}, u32[]{:S(2)}) %all-to-all-start) | async-done | bytes 6291488 | tf_op jit(solution)/shard_map/all_to_all | solution.py:26
  167.4 16.0 %fusion.5 = f32[1536,2048]{1,0:T(8,128)} fusion(bf16[1536,1536]{0,1:T(8,128)(2,1)} %all-gather.2.cloned.1.call-done, bf16[2048,1536]{0,1:T(8,128)(2,1)} %bitcast.5), kind=kOutput, calls=%fused_computation.20 | convolution fusion | flops 9663676416 | bytes 23592960 | tf_op jit(solution)/shard_map/dot_general | solution.py:18
  183.4 107.4 %reduce-scatter.2.cloned.1.call-done = f32[384,2048]{1,0:T(8,128)} async-done(((f32[1536,2048]{1,0:T(8,128)}), f32[384,2048]{1,0:T(8,128)}) %reduce-scatter.2.cloned.1.call-update) | async-done | bytes 3145744 | tf_op jit(solution)/shard_map/reduce_scatter | solution.py:34
  290.8 3.3 %convert_element_type.27 = bf16[384,2048]{1,0:T(8,128)(2,1)} convert(f32[384,2048]{1,0:T(8,128)} %reduce-scatter.2.cloned.1.call-done) | non-fusion elementwise | flops 786432 | bytes 4718592 | tf_op jit(solution)/shard_map/convert_element_type | solution.py:35
  (11 shorter events, 0.1 us)
Async XLA Ops:
  6.5 6.2 %copy-start = (bf16[2048,192]{0,1:T(8,128)(2,1)S(1)}, bf16[2048,192]{0,1:T(8,128)(2,1)}, u32[]{:S(2)}) copy-start(bf16[2048,192]{0,1:T(8,128)(2,1)} %param.4) | copy-start | bytes 2359300
  13.6 2.7 copy-start.1
  16.2 9.2 %copy-start.3 = (s32[16,16]{1,0:T(8,128)S(1)}, s32[16,16]{1,0:T(8,128)}, u32[]{:S(2)}) copy-start(s32[16,16]{1,0:T(8,128)} %param.7) | copy-start | bytes 3076
  16.2 10.8 %copy-start.2 = (bf16[1536,192]{0,1:T(8,128)(2,1)S(1)}, bf16[1536,192]{0,1:T(8,128)(2,1)}, u32[]{:S(2)}) copy-start(bf16[1536,192]{0,1:T(8,128)(2,1)} %param.5) | copy-start | bytes 1769476
  16.2 151.1 %all-to-all-start = ((bf16[2048,8,192]{0,2,1:T(8,128)(2,1)}), bf16[2048,8,192]{0,2,1:T(8,128)(2,1)}, u32[]{:S(2)}, u32[]{:S(2)}) async-start(bf16[2048,8,192]{0,2,1:T(8,128)(2,1)} %bitcast.13), calls=%async_computation | async-start | bytes 12582912 | tf_op jit(solution)/shard_map/all_to_all | solution.py:26
  25.4 64.8 %all-gather.2.cloned.1.call-start = ((), (), s32[]{:S(2)}) async-start(), calls=%async_computation.2 | async-start | bytes 5308416 | tf_op jit(solution)/shard_map/all_gather | solution.py:33
  28.1 262.8 %reduce-scatter.2.cloned.1.call-start = ((), (), s32[]{:S(2)}) async-start(), calls=%async_computation.3 | async-start | bytes 15728640 | tf_op jit(solution)/shard_map/reduce_scatter | solution.py:34
Sparse Core Ops, SparseCore 0:
  28.2 61.9 all-gather.1
  183.6 107.2 reduce-scatter.1
